TPU v7x, 128 devices: a whole 4x4x4 slice. The times are simulated.
128 devices in a mesh: row: 16 (over y, z_hi, core), col: 8 (over x, z_lo).
Axes of the slice: x: 4, y: 4, z: 4 (z_hi: 2, z_lo: 2; z = z_hi * 2 + z_lo), core: 2. Of those that a mesh axis runs over, the one named last changes fastest.
Arguments:
- orbitals: bfloat16 [24576, 2, 2048], P(('row', 'col')), may hold values from -6 to 6
- applied_orbitals: bfloat16 [24576, 2, 2048], P(('row', 'col')), may hold values from -6 to 6
- ritz_matrix: bfloat16 [2, 2048, 2048], P(None, 'row', 'col'), may hold values from -0.09375 to 0.09375
Outputs:
- rotated_orbitals: bfloat16 [24576, 2, 2048], P(('row', 'col'))
- rotated_applied: bfloat16 [24576, 2, 2048], P(('row', 'col'))
All inputs are finite; a program needn't handle non-finite values.
Results may differ from a plain program's by a relative error of at most 0.001.
Values may be sent and summed in bfloat16 or wider, within the bound.
A program may use at most 128 MiB of HBM per device.

v0:
```python
import jax
import jax.numpy as jnp
from jax import lax
from jax.sharding import PartitionSpec as P


def shards(orbitals, applied_orbitals, ritz_matrix):
    row_count = orbitals.shape[0]
    band_count = orbitals.shape[2]
    stacked = jnp.concatenate(
        [
            orbitals.reshape(row_count, 2 * band_count),
            applied_orbitals.reshape(row_count, 2 * band_count),
        ],
        0,
    )
    strip = lax.all_gather(ritz_matrix, "col", axis=2, tiled=True)
    shard_piece = lax.all_gather(strip, "row", axis=1, tiled=True)
    height = shard_piece.shape[1]
    real_cols = lax.slice_in_dim(stacked, 0, height, axis=1)
    imag_cols = lax.dynamic_slice_in_dim(stacked, band_count, height, 1)
    upper_half = jnp.concatenate([shard_piece[0], shard_piece[1]], 1)
    lower_half = jnp.concatenate([-shard_piece[1], shard_piece[0]], 1)
    running = jnp.dot(real_cols, upper_half, preferred_element_type=jnp.float32)
    running = running + jnp.dot(imag_cols, lower_half, preferred_element_type=jnp.float32)
    result = running.reshape(2 * row_count, 2, band_count)
    result = result.astype(jnp.bfloat16)
    return (result[:row_count], result[row_count:])


def solution(mesh):
    in_specs = (P(("row", "col"), None, None), P(("row", "col"), None, None), P(None, "row", "col"))
    out_specs = (P(("row", "col"), None, None), P(("row", "col"), None, None))
    return jax.shard_map(shards, mesh=mesh, in_specs=in_specs, out_specs=out_specs, check_vma=False)
```

profile of v0, /device:TPU:1, one launch (start us, length us, event | category | flops | bytes accessed | tf_op | source)
XLA Modules:
  0.0 229.9 jit_solution(4716080918865581641)
XLA Ops:
  7.2 0.0 all-gather.3.cloned.1.call-start
  7.2 0.7 all-gather.3.cloned.1.call-update
  7.9 0.0 all-gather.5.cloned.1.call-start
  7.9 43.9 %all-gather.3.cloned.1.call-done = bf16[2,128,2048]{2,1,0:T(8,128)(2,1)} async-done(((bf16[2,128,256]{2,1,0:T(8,128)(2,1)}), bf16[2,128,2048]{2,1,0:T(8,128)(2,1)}) %all-gather.3.cloned.1.call-update) | async-done | bytes 1048592 | tf_op jit(solution)/shard_map/all_gather | solution.py:17
  51.8 0.0 all-gather.5.cloned.1.call-update
  51.8 2.1 copy.5
  53.9 2.1 copy.6
  55.9 0.1 constant_dynamic-update-slice_fusion.1
  56.1 0.1 constant_dynamic-update-slice_fusion
  56.2 114.2 %all-gather.5.cloned.1.call-done = bf16[2,2048,2048]{2,1,0:T(8,128)(2,1)} async-done(((bf16[2,128,2048]{2,1,0:T(8,128)(2,1)}), bf16[2,2048,2048]{2,1,0:T(8,128)(2,1)}) %all-gather.5.cloned.1.call-update) | async-done | bytes 16777232 | tf_op jit(solution)/shard_map/all_gather | solution.py:18
  170.4 11.8 %slice_bitcast_fusion.1 = (bf16[2048,2048]{1,0:T(8,128)(2,1)}, bf16[2048,2048]{1,0:T(8,128)(2,1)}) fusion(bf16[2,2048,2048]{2,1,0:T(8,128)(2,1)} %all-gather.5.cloned.1.call-done), kind=kLoop, calls=%fused_computation.9 | loop fusion | bytes 33554432 | tf_op jit(solution)/shard_map/squeeze | solution.py:22
  182.2 12.6 %fusion = f32[384,4096]{1,0:T(8,128)} fusion(bf16[2048,2048]{1,0:T(8,128)(2,1)} %get-tuple-element.3, bf16[2048,2048]{1,0:T(8,128)(2,1)} %get-tuple-element.2, bf16[384,4096]{1,0:T(8,128)(2,1)S(1)} %constant_dynamic-update-slice_fusion), kind=kOutput, calls=%fused_computation | convolution fusion | flops 6476005376 | bytes 24641536 | tf_op jit(solution)/shard_map/dot_general | solution.py:24
  194.8 7.1 %fusion.14 = bf16[2048,2048]{1,0:T(8,128)(2,1)} fusion(bf16[2,2048,2048]{2,1,0:T(8,128)(2,1)} %all-gather.5.cloned.1.call-done), kind=kLoop, calls=%fused_computation.17 | loop fusion | flops 4194304 | bytes 16777216 | tf_op jit(solution)/shard_map/neg | solution.py:23
  201.9 14.3 %add_convert_fusion = bf16[384,4096]{1,0:T(8,128)(2,1)} fusion(f32[384,4096]{1,0:T(8,128)} %fusion, bf16[2048,2048]{1,0:T(8,128)(2,1)} %get-tuple-element.2, bf16[2048,2048]{1,0:T(8,128)(2,1)} %fusion.14, bf16[384,4096]{1,0:T(8,128)(2,1)S(1)} %constant_dynamic-update-slice_fusion), kind=kOutput, calls=%fused_computation.10 | convolution fusion | flops 6479151104 | bytes 27787264 | tf_op jit(solution)/shard_map/dot_general | solution.py:25
  216.2 2.1 fusion.15
  218.3 2.4 %slice.27 = bf16[192,2,2048]{2,1,0:T(2,128)(2,1)} reshape(bf16[192,4096]{1,0:T(8,128)(2,1)S(1)} %get-tuple-element.5) | data formatting | bytes 3145728 | tf_op jit(solution)/shard_map/slice | solution.py:28
  220.7 2.4 %slice.29 = bf16[192,2,2048]{2,1,0:T(2,128)(2,1)} reshape(bf16[192,4096]{1,0:T(8,128)(2,1)S(1)} %get-tuple-element.4) | data formatting | bytes 3145728 | tf_op jit(solution)/shard_map/slice | solution.py:28
Async XLA Ops:
  7.2 44.6 %all-gather.3.cloned.1.call-start = ((), (), s32[]{:S(2)}) async-start(), calls=%async_computation | async-start | bytes 1179648 | tf_op jit(solution)/shard_map/all_gather | solution.py:17
  7.9 162.5 %all-gather.5.cloned.1.call-start = ((), (), s32[]{:S(2)}) async-start(), calls=%async_computation.1 | async-start | bytes 17825792 | tf_op jit(solution)/shard_map/all_gather | solution.py:18
Sparse Core Ops, SparseCore 0:
  9.6 42.1 all-gather.2
  54.3 116.0 all-gather.4
where the time goes:
time: 230 us
  waiting for transfers between devices  159 us (69%)
  matrix products  26.9 us (12%)
  local copies, waits for them, and re-layouts  23 us (10%)
  between operations  14.1 us (6%)
  other arithmetic  7.14 us (3%)
    all_gather x1, waiting for transfers between devices, shards(): shard_piece = lax.all_gather(strip, 'row', axis=1, tiled=True)  114 us
    all_gather x1, waiting for transfers between devices, shards(): strip = lax.all_gather(ritz_matrix, 'col', axis=2, tiled=True)  43.9 us
    dot_general x1, matrix products, shards(): jnp.dot(imag_cols, lower_half, preferred_element_type=jnp.float32)  14.3 us
    dot_general x1, matrix products, shards(): running = jnp.dot(real_cols, upper_half, preferred_element_type=jnp.float32)  12.6 us
    squeeze x1, local copies, waits for them, and re-layouts, shards(): upper_half = jnp.concatenate([shard_piece[0], shard_piece[1]], 1)  11.8 us
    neg x1, other arithmetic, shards(): lower_half = jnp.concatenate([-shard_piece[1], shard_piece[0]], 1)  7.14 us
    slice x3, local copies, waits for them, and re-layouts, shards(): return (result[:row_count], result[row_count:])  6.8 us
  transfers between devices with their start and end apart: 2, of which 2 were waited for; matrix products, arithmetic and copies ran while one was open for 2% of the time, Pallas kernels for 0%

commit v1 on v0

--- a/solution.py
+++ b/solution.py
@@ -14,7 +14,9 @@
         ],
         0,
     )
-    strip = lax.all_gather(ritz_matrix, "col", axis=2, tiled=True)
+    strip = jnp.concatenate(
+        lax.all_to_all(jnp.stack([ritz_matrix] * lax.axis_size("col")), "col", 0, 0), axis=2
+    )
     shard_piece = lax.all_gather(strip, "row", axis=1, tiled=True)
     height = shard_piece.shape[1]
     real_cols = lax.slice_in_dim(stacked, 0, height, axis=1)

time: 230 us -> 216 us (0.939)
  waiting for transfers between devices: 159 us -> 124 us
  blocking collectives: 0 us -> 20.3 us
    all_gather x1 -> x0, waiting for transfers between devices: 43.9 us -> none  [shards(): strip = lax.all_gather(ritz_matrix, 'col', axis=2, tiled=True)]
    all_to_all x0 -> x1, blocking collectives: none -> 20.3 us  [shards(): lax.all_to_all(jnp.stack([ritz_matrix] * lax.axis_size('col')), 'col', 0, 0)]
    all_gather x1, waiting for transfers between devices: 114 us -> 124 us  [shards(): shard_piece = lax.all_gather(strip, 'row', axis=1, tiled=True)]
  transfers between devices with their start and end apart: 2 -> 1, of which waited for: 2 -> 1; matrix products, arithmetic and copies ran while one was open for 2% -> 1% of each run, Pallas kernels for 0% -> 0%
where the time goes in v1:
time: 216 us
  waiting for transfers between devices  124 us (57%)
  matrix products  27.1 us (13%)
  local copies, waits for them, and re-layouts  22.6 us (10%)
  blocking collectives  20.3 us (9%)
  between operations  14.1 us (7%)
  other arithmetic  7.15 us (3%)
    all_gather x1, waiting for transfers between devices, shards(): shard_piece = lax.all_gather(strip, 'row', axis=1, tiled=True)  124 us
    all_to_all x1, blocking collectives, shards(): lax.all_to_all(jnp.stack([ritz_matrix] * lax.axis_size('col')), 'col', 0, 0)  20.3 us
    dot_general x1, matrix products, shards(): jnp.dot(imag_cols, lower_half, preferred_element_type=jnp.float32)  14.4 us
    dot_general x1, matrix products, shards(): running = jnp.dot(real_cols, upper_half, preferred_element_type=jnp.float32)  12.7 us
    squeeze x1, local copies, waits for them, and re-layouts, shards(): upper_half = jnp.concatenate([shard_piece[0], shard_piece[1]], 1)  11.8 us
    neg x1, other arithmetic, shards(): lower_half = jnp.concatenate([-shard_piece[1], shard_piece[0]], 1)  7.15 us
    slice x3, local copies, waits for them, and re-layouts, shards(): return (result[:row_count], result[row_count:])  6.8 us
  transfers between devices with their start and end apart: 1, of which 1 were waited for; matrix products, arithmetic and copies ran while one was open for 1% of the time, Pallas kernels for 0%

profile of v1, /device:TPU:1, one launch (start us, length us, event | category | flops | bytes accessed | tf_op | source)
XLA Modules:
  0.0 215.5 jit_solution(11595532196975396021)
XLA Ops:
  7.2 0.0 copy-start
  7.2 0.0 copy-start.1
  7.2 0.0 all-gather.2.cloned.1.call-start
  7.2 1.2 copy.6
  8.4 0.2 stack.2
  8.6 20.3 %all_to_all.5 = bf16[8,2,128,256]{2,3,1,0:T(8,128)(2,1)S(1)} all-to-all(bf16[8,2,128,256]{2,3,1,0:T(8,128)(2,1)S(1)} %stack.2), channel_id=1, replica_groups=mesh['row'=16,'col'=8] {'col'}, dimensions={0} | all-to-all | bytes 2097152 | tf_op jit(solution)/shard_map/all_to_all | solution.py:18
  28.9 1.0 copy.7
  30.0 0.0 all-gather.2.cloned.1.call-update
  30.0 0.0 copy-done
  30.0 0.6 copy.8
  30.7 0.0 copy-done.1
  30.7 0.6 copy.9
  31.3 0.1 constant_dynamic-update-slice_fusion.1
  31.5 0.1 constant_dynamic-update-slice_fusion
  31.6 124.2 %all-gather.2.cloned.1.call-done = bf16[2,2048,2048]{1,2,0:T(8,128)(2,1)} async-done(((bf16[2,128,2048]{1,2,0:T(8,128)(2,1)}), bf16[2,2048,2048]{1,2,0:T(8,128)(2,1)}) %all-gather.2.cloned.1.call-update) | async-done | bytes 16777232 | tf_op jit(solution)/shard_map/all_gather | solution.py:20
  155.8 11.8 %slice_bitcast_fusion.1 = (bf16[2048,2048]{0,1:T(8,128)(2,1)}, bf16[2048,2048]{0,1:T(8,128)(2,1)}) fusion(bf16[2,2048,2048]{1,2,0:T(8,128)(2,1)} %all-gather.2.cloned.1.call-done), kind=kLoop, calls=%fused_computation.9 | loop fusion | bytes 33554432 | tf_op jit(solution)/shard_map/squeeze | solution.py:24
  167.6 12.7 %fusion = f32[384,4096]{1,0:T(8,128)} fusion(bf16[2048,2048]{0,1:T(8,128)(2,1)} %get-tuple-element.3, bf16[2048,2048]{0,1:T(8,128)(2,1)} %get-tuple-element.2, bf16[384,4096]{1,0:T(8,128)(2,1)S(1)} %constant_dynamic-update-slice_fusion), kind=kOutput, calls=%fused_computation | convolution fusion | flops 6476005376 | bytes 24641536 | tf_op jit(solution)/shard_map/dot_general | solution.py:26
  180.3 7.1 %fusion.14 = bf16[2048,2048]{0,1:T(8,128)(2,1)} fusion(bf16[2,2048,2048]{1,2,0:T(8,128)(2,1)} %all-gather.2.cloned.1.call-done), kind=kLoop, calls=%fused_computation.17 | loop fusion | flops 4194304 | bytes 16777216 | tf_op jit(solution)/shard_map/neg | solution.py:25
  187.5 14.4 %add_convert_fusion = bf16[384,4096]{1,0:T(8,128)(2,1)} fusion(f32[384,4096]{1,0:T(8,128)} %fusion, bf16[2048,2048]{0,1:T(8,128)(2,1)} %get-tuple-element.2, bf16[2048,2048]{0,1:T(8,128)(2,1)} %fusion.14, bf16[384,4096]{1,0:T(8,128)(2,1)S(1)} %constant_dynamic-update-slice_fusion), kind=kOutput, calls=%fused_computation.10 | convolution fusion | flops 6479151104 | bytes 27787264 | tf_op jit(solution)/shard_map/dot_general | solution.py:27
  201.9 2.1 fusion.15
  204.0 2.4 %slice.27 = bf16[192,2,2048]{2,1,0:T(2,128)(2,1)} reshape(bf16[192,4096]{1,0:T(8,128)(2,1)S(1)} %get-tuple-element.5) | data formatting | bytes 3145728 | tf_op jit(solution)/shard_map/slice | solution.py:30
  206.4 2.4 %slice.29 = bf16[192,2,2048]{2,1,0:T(2,128)(2,1)} reshape(bf16[192,4096]{1,0:T(8,128)(2,1)S(1)} %get-tuple-element.4) | data formatting | bytes 3145728 | tf_op jit(solution)/shard_map/slice | solution.py:30
Async XLA Ops:
  7.2 22.8 %copy-start = (bf16[192,2,2048]{2,1,0:T(2,128)(2,1)S(1)}, bf16[192,2,2048]{2,1,0:T(2,128)(2,1)}, u32[]{:S(2)}) copy-start(bf16[192,2,2048]{2,1,0:T(2,128)(2,1)} %param.3) | copy-start | bytes 4718596
  7.2 23.5 %copy-start.1 = (bf16[192,2,2048]{2,1,0:T(2,128)(2,1)S(1)}, bf16[192,2,2048]{2,1,0:T(2,128)(2,1)}, u32[]{:S(2)}) copy-start(bf16[192,2,2048]{2,1,0:T(2,128)(2,1)} %param.4) | copy-start | bytes 4718596
  7.2 148.6 %all-gather.2.cloned.1.call-start = ((), (), s32[]{:S(2)}) async-start(), calls=%async_computation.1 | async-start | bytes 17825792 | tf_op jit(solution)/shard_map/all_gather | solution.py:20
Sparse Core Ops, SparseCore 0:
  30.1 125.6 all-gather.1
